TPU v7x, 32 devices: a whole 2x2x4 slice. The times are simulated.
32 devices in a mesh: row: 4 (over z), col: 8 (over y, x, core).
Axes of the slice: x: 2, y: 2, z: 4, core: 2. Of those that a mesh axis runs over, the one named last changes fastest.
Arguments:
- load_amp: float32 [2048, 4096], P('row', 'col'), may hold values from 0.05 to 1
- load_mask: int32 [2048, 4096], P('row', 'col'), may hold values 0 or 1
- leak: float32 [2048, 4096], P('row', 'col'), may hold values from 0.001 to 0.05
- coarse_leak: float32 [512, 1024], P('row', 'col'), may hold values from 0.01 to 0.5
- coarse_init: float32 [512, 1024], P('row', 'col'), may hold values from 0 to 1
- via_fine: int32 [4, 8192], P('row', 'col'), may hold values from 0 to 262143
- via_coarse: int32 [4, 8192], P('row', 'col'), may hold values from 0 to 131071, as said below
- via_count: int32 [4, 64], P('row', 'col'), may hold values from 0 to 128, as said below
Outputs:
- fine_drop: float32 [2048, 4096], P('row', 'col')
- coarse_drop: float32 [512, 1024], P('row', 'col')
Inputs may be any that keep to these rules, and one draw needn't show every extreme that they name: `via_coarse`: slot s of a tile names a coarse node whose stored column lies in s // 128 * 128 to s // 128 * 128 + 127. `via_count`: slots of an owner past its count are padding and carry arbitrary indices. In each tile row some owner gets 128 live slots from every tile of that row.
All inputs are finite; a program needn't handle non-finite values. No bound on the sum of `load_mask` on one device may be relied on, other than what follows from the above.
Results may differ from a plain program's by a relative error of at most 0.00022.
Values sent between devices are 32-bit elements; how exact they have to be, the bound alone decides.
A program may use at most 64 MiB of HBM per device.

v0:
```python
import jax
import jax.numpy as jnp
from jax import lax
from jax.sharding import PartitionSpec as P

GROUP = 16
ITERS = 4
CSWEEP = 2
via_conductance = 2.0
coarse_conductance = 4.0
relaxation = 0.8


def extended(block, sides, width, periodic):
    for axis, dim in sides:
        count = lax.axis_size(axis)
        forward = [(i, i + 1) for i in range(count - 1)]
        if periodic:
            forward.append((count - 1, 0))
        backward = [(target, source) for source, target in forward]
        low = lax.ppermute(
            lax.slice_in_dim(block, block.shape[dim] - width, None, axis=dim), axis, forward
        )
        high = lax.ppermute(lax.slice_in_dim(block, 0, width, axis=dim), axis, backward)
        block = jnp.concatenate([low, block, high], axis=dim)
    return block


def fine_apply(field, diagonal):
    padded = extended(field, (("row", 0), ("col", 1)), 1, False)
    beside = padded[2:, 1:-1] + padded[:-2, 1:-1] + padded[1:-1, 2:] + padded[1:-1, :-2]
    return diagonal * field - beside


def coarse_apply(volt, diagonal):
    block_rows, block_cols = volt.shape
    groups = block_cols // GROUP
    stacked = extended(volt, (("row", 0),), 1, False)
    up_down = stacked[2:] + stacked[:-2]
    grouped = volt.reshape(block_rows, groups, GROUP)
    seam = jnp.stack([grouped[:, :, 0], grouped[:, :, GROUP - 1]], axis=0)
    edges = extended(seam, (("col", 0),), 1, True)
    from_left = edges[0]
    from_right = edges[3]
    place = lax.axis_index("col")
    width = lax.axis_size("col")
    zero_col = jnp.zeros((block_rows, 1), jnp.float32)
    left_turned = jnp.concatenate([zero_col, from_left[:, :-1]], axis=1)
    from_left = jnp.where(place == 0, left_turned, from_left)
    right_turned = jnp.concatenate([from_right[:, 1:], zero_col], axis=1)
    from_right = jnp.where(place == width - 1, right_turned, from_right)
    left_full = jnp.concatenate([from_left[:, :, None], grouped[:, :, :-1]], axis=2).reshape(
        block_rows, block_cols
    )
    right_full = jnp.concatenate([grouped[:, :, 1:], from_right[:, :, None]], axis=2).reshape(
        block_rows, block_cols
    )
    return diagonal * volt - coarse_conductance * (up_down + left_full + right_full)


def paired_sum(first, second):
    return lax.psum((jnp.sum(first), jnp.sum(second)), ("row", "col"))


def per_device(
    load_amp, load_mask, leak, coarse_leak, coarse_init, via_fine, via_coarse, via_count
):
    tile_rows, tile_cols = leak.shape
    block_rows, block_cols = coarse_leak.shape
    owners = lax.axis_size("col")
    slot_count = via_fine.shape[1]
    per_owner = slot_count // owners
    row_width = block_cols * owners
    slot_all = jnp.arange(slot_count, dtype=jnp.int32)
    position = slot_all % per_owner
    live = position < jnp.repeat(via_count[0], per_owner)
    weight = jnp.where(live, via_conductance, 0.0).astype(jnp.float32)
    fine_index = via_fine[0]
    coarse_index = via_coarse[0]
    via_diag = jnp.zeros(tile_rows * tile_cols, jnp.float32).at[fine_index].add(weight)
    fine_diag = 4.0 + leak + via_diag.reshape(tile_rows, tile_cols)
    count_local = jnp.zeros(block_rows * row_width, jnp.float32).at[coarse_index].add(weight)
    coarse_count = lax.psum_scatter(
        count_local.reshape(block_rows, row_width), "col", scatter_dimension=1, tiled=True
    )
    coarse_diag = 4.0 * coarse_conductance + coarse_leak + coarse_count
    load = load_amp * load_mask.astype(jnp.float32)
    volt = coarse_init
    solution = jnp.zeros((tile_rows, tile_cols), jnp.float32)
    gathered = lax.all_gather(volt, "col", axis=1, tiled=True)
    at_via = gathered.reshape(-1)[coarse_index]
    injected = jnp.zeros(tile_rows * tile_cols, jnp.float32).at[fine_index].add(weight * at_via)
    rhs = load + injected.reshape(tile_rows, tile_cols)
    residual = rhs - fine_apply(solution, fine_diag)
    precond = residual / fine_diag
    image = fine_apply(precond, fine_diag)
    product, curvature = paired_sum(residual * precond, image * precond)
    alpha = product / curvature
    direction = precond
    along = image
    for iteration in range(ITERS):
        solution = solution + alpha * direction
        residual = residual - alpha * along
        if iteration + 1 < ITERS:
            precond = residual / fine_diag
            image = fine_apply(precond, fine_diag)
            renewed, curvature = paired_sum(residual * precond, image * precond)
            ratio = renewed / product
            alpha = renewed / (curvature - ratio * renewed / alpha)
            direction = precond + ratio * direction
            along = image + ratio * along
            product = renewed
    at_fine = weight * solution.reshape(-1)[fine_index]
    partial_block = jnp.zeros(block_rows * row_width, jnp.float32).at[coarse_index].add(at_fine)
    sources = lax.psum_scatter(
        partial_block.reshape(block_rows, row_width), "col", scatter_dimension=1, tiled=True
    )
    for sweep_turn in range(CSWEEP):
        volt = volt + relaxation * (sources - coarse_apply(volt, coarse_diag)) / coarse_diag
    return (solution, volt)


def solution(mesh):
    in_specs = (
        P("row", "col"),
        P("row", "col"),
        P("row", "col"),
        P("row", "col"),
        P("row", "col"),
        P("row", "col"),
        P("row", "col"),
        P("row", "col"),
    )
    out_specs = (P("row", "col"), P("row", "col"))
    return jax.shard_map(
        per_device, mesh=mesh, in_specs=in_specs, out_specs=out_specs, check_vma=False
    )
```

profile of v0, /device:TPU:0, one launch (start us, length us, event | category | flops | bytes accessed | tf_op | source)
XLA Modules:
  0.0 400.2 jit_solution(1084697743863416688)
XLA Ops:
  8.5 5.6 %collective-permute-start.1 = (f32[1,512]{1,0:T(1,128)S(1)}, f32[1,512]{1,0:T(1,128)S(1)}, u32[]{:S(2)}, u32[]{:S(2)}) collective-permute-start(f32[1,512]{1,0:T(1,128)S(1)} %broadcast.77), channel_id=1, source_target_pairs={{0,8},{8,16},{16,24},{1,9},{9,17},{17,25},{2,10},{10,18},{18,26},{... | collective-permute-start | bytes 6152 | tf_op jit(solution)/shard_map/ppermute | solution.py:21
  14.8 11.7 %all_gather.3 = f32[128,1024]{1,0:T(8,128)S(1)} all-gather(f32[128,128]{1,0:T(8,128)} %param.12), channel_id=1, replica_groups=mesh['row'=4,'col'=8] {'col'}, dimensions={1}, use_global_device_ids=true | all-gather | bytes 589824 | tf_op jit(solution)/shard_map/all_gather | solution.py:90
  26.6 6.2 %gather_fusion = f32[1024]{0:T(1024)S(1)} fusion(f32[131072]{0:T(1024)S(1)} %bitcast.53, s32[1024]{0:T(1024)S(1)} %broadcast_clamp_fusion.1), kind=kCustom, calls=%fused_computation | custom fusion | bytes 12288 | tf_op jit(solution)/shard_map/gather | solution.py:91
  34.4 3.7 collective-permute-start.3
  38.2 6.2 %scatter_custom_fusion.1 = f32[262144]{0:T(1024)S(1)} fusion(s32[1024]{0:T(1024)S(1)} %bitcast.75, f32[1024]{0:T(1024)S(1)} %get-tuple-element.61, f32[]{:T(128)} %constant.12.clone.1), kind=kCustom, calls=%fused_computation.82 | custom fusion | flops 1024 | bytes 1048580 | tf_op jit(solution)/shard_map/scatter-add | solution.py:80
  45.6 6.2 %scatter_custom_fusion = f32[262144]{0:T(1024)S(1)} fusion(s32[1024]{0:T(1024)S(1)} %bitcast.76, f32[1024]{0:T(1024)S(1)} %get-tuple-element.62, f32[]{:T(128)} %constant.12.clone.1), kind=kCustom, calls=%fused_computation.84 | custom fusion | flops 1024 | bytes 1048580 | tf_op jit(solution)/shard_map/scatter-add | solution.py:92
  52.9 3.4 fusion.61
  57.6 4.5 %collective-permute-start.5 = (f32[1,512]{1,0:T(1,128)S(1)}, f32[1,512]{1,0:T(1,128)S(1)}, u32[]{:S(2)}, u32[]{:S(2)}) collective-permute-start(f32[1,512]{1,0:T(1,128)S(1)} %get-tuple-element.47), channel_id=1, source_target_pairs={{0,8},{8,16},{16,24},{1,9},{9,17},{17,25},{2,10},{10,18},{18,26},{... | collective-permute-start | bytes 6152 | tf_op jit(solution)/shard_map/ppermute | solution.py:21
  64.9 3.0 collective-permute-start.7
  70.5 46.7 %all-reduce.9 = (f32[]{:T(128)}, f32[]{:T(128)}) all-reduce(f32[]{:T(128)} %get-tuple-element.11, f32[]{:T(128)} %get-tuple-element.10), channel_id=1, replica_groups=mesh['row'=4,'col'=8] {'row','col'}, use_global_device_ids=true, to_apply=%region_3.4 | all-reduce | flops 2 | bytes 16 | tf_op jit(solution)/shard_map/psum | solution.py:62
  121.5 4.5 %collective-permute-start.9 = (f32[1,512]{1,0:T(1,128)S(1)}, f32[1,512]{1,0:T(1,128)S(1)}, u32[]{:S(2)}, u32[]{:S(2)}) collective-permute-start(f32[1,512]{1,0:T(1,128)S(1)} %get-tuple-element.45), channel_id=1, source_target_pairs={{0,8},{8,16},{16,24},{1,9},{9,17},{17,25},{2,10},{10,18},{18,26},{... | collective-permute-start | bytes 6152 | tf_op jit(solution)/shard_map/ppermute | solution.py:21
  128.8 3.0 collective-permute-start.11
  133.0 2.4 multiply_reduce_fusion.3
  135.4 46.5 %all-reduce.8 = (f32[]{:T(128)}, f32[]{:T(128)}) all-reduce(f32[]{:T(128)} %get-tuple-element.9, f32[]{:T(128)} %get-tuple-element.8), channel_id=1, replica_groups=mesh['row'=4,'col'=8] {'row','col'}, use_global_device_ids=true, to_apply=%region_7.8 | all-reduce | flops 2 | bytes 16 | tf_op jit(solution)/shard_map/psum | solution.py:62
  186.4 3.0 fusion.57
  190.7 4.5 %collective-permute-start.13 = (f32[1,512]{1,0:T(1,128)S(1)}, f32[1,512]{1,0:T(1,128)S(1)}, u32[]{:S(2)}, u32[]{:S(2)}) collective-permute-start(f32[1,512]{1,0:T(1,128)S(1)} %get-tuple-element.43), channel_id=1, source_target_pairs={{0,8},{8,16},{16,24},{1,9},{9,17},{17,25},{2,10},{10,18},{18,26},{... | collective-permute-start | bytes 6152 | tf_op jit(solution)/shard_map/ppermute | solution.py:21
  198.7 3.8 collective-permute-start.15
  204.7 7.0 %scatter_custom_fusion.3 = f32[131072]{0:T(1024)} fusion(s32[1024]{0:T(1024)} %bitcast.73, f32[1024]{0:T(1024)} %copy-done.14, f32[]{:T(128)} %constant.12.clone.1), kind=kCustom, calls=%fused_computation.101 | custom fusion | flops 1024 | bytes 524800 | tf_op jit(solution)/shard_map/scatter-add | solution.py:82
  211.7 1.9 reshape.105
  213.7 2.4 multiply_reduce_fusion.1
  216.1 41.9 %all-reduce.7 = (f32[]{:T(128)}, f32[]{:T(128)}) all-reduce(f32[]{:T(128)} %get-tuple-element.7, f32[]{:T(128)} %get-tuple-element.6), channel_id=1, replica_groups=mesh['row'=4,'col'=8] {'row','col'}, use_global_device_ids=true, to_apply=%region_11.12 | all-reduce | flops 2 | bytes 16 | tf_op jit(solution)/shard_map/psum | solution.py:62
  261.8 2.7 fusion.56
  265.9 4.5 %collective-permute-start.17 = (f32[1,512]{1,0:T(1,128)S(1)}, f32[1,512]{1,0:T(1,128)S(1)}, u32[]{:S(2)}, u32[]{:S(2)}) collective-permute-start(f32[1,512]{1,0:T(1,128)S(1)} %get-tuple-element.41), channel_id=1, source_target_pairs={{0,8},{8,16},{16,24},{1,9},{9,17},{17,25},{2,10},{10,18},{18,26},{... | collective-permute-start | bytes 6152 | tf_op jit(solution)/shard_map/ppermute | solution.py:21
  273.8 3.0 collective-permute-start.19
  276.9 5.1 %collective-permute-start.21 = (f32[1,128]{1,0:T(1,128)}, f32[1,128]{1,0:T(1,128)}, u32[]{:S(2)}, u32[]{:S(2)}) collective-permute-start(f32[1,128]{1,0:T(1,128)} %get-tuple-element.56), channel_id=1, source_target_pairs={{0,8},{8,16},{16,24},{1,9},{9,17},{17,25},{2,10},{10,18},{18,26},{... | collective-permute-start | bytes 1544 | tf_op jit(solution)/shard_map/ppermute | solution.py:21
  283.4 43.5 %all-reduce.6 = (f32[]{:T(128)}, f32[]{:T(128)}) all-reduce(f32[]{:T(128)} %get-tuple-element.5, f32[]{:T(128)} %get-tuple-element.4), channel_id=1, replica_groups=mesh['row'=4,'col'=8] {'row','col'}, use_global_device_ids=true, to_apply=%region_15.16 | all-reduce | flops 2 | bytes 16 | tf_op jit(solution)/shard_map/psum | solution.py:62
  330.6 2.1 multiply_add_fusion
  333.7 6.1 %gather_fusion.1 = f32[1024]{0:T(1024)S(1)} fusion(f32[262144]{0:T(1024)S(1)} %bitcast.54, s32[1024]{0:T(1024)S(1)} %broadcast_clamp_fusion), kind=kCustom, calls=%fused_computation.1 | custom fusion | bytes 12288 | tf_op jit(solution)/shard_map/gather | solution.py:113
  339.9 6.2 %scatter_custom_fusion.2 = f32[131072]{0:T(1024)S(1)} fusion(s32[1024]{0:T(1024)} %bitcast.74, f32[1024]{0:T(1024)S(1)} %fusion.54, f32[]{:T(128)} %constant.12.clone.1), kind=kCustom, calls=%fused_computation.103 | custom fusion | flops 1024 | bytes 524800 | tf_op jit(solution)/shard_map/scatter-add | solution.py:114
  348.8 33.0 %reduce-scatter.3.cloned.1.call-done = f32[128,128]{1,0:T(8,128)} async-done(((f32[128,1024]{1,0:T(8,128)}), f32[128,128]{1,0:T(8,128)}) %reduce-scatter.3.cloned.1.call-update) | async-done | bytes 65552 | tf_op jit(solution)/shard_map/reduce_scatter | solution.py:115
  383.0 2.6 collective-permute-start.27
  386.9 4.5 %collective-permute-start.25 = (f32[1,128]{1,0:T(1,128)S(1)}, f32[1,128]{1,0:T(1,128)S(1)}, u32[]{:S(2)}, u32[]{:S(2)}) collective-permute-start(f32[1,128]{1,0:T(1,128)S(1)} %get-tuple-element.50), channel_id=1, source_target_pairs={{0,8},{8,16},{16,24},{1,9},{9,17},{17,25},{2,10},{10,18},{18,26},{... | collective-permute-start | bytes 1544 | tf_op jit(solution)/shard_map/ppermute | solution.py:21
  (132 shorter events, 40.3 us)
Async XLA Ops:
  7.2 341.6 %reduce-scatter.5.cloned.1.call-start = ((), (), s32[]{:S(2)}) async-start(), calls=%async_computation.3 | async-start | bytes 589824 | tf_op jit(solution)/shard_map/reduce_scatter | solution.py:83
  7.2 25.6 %collective-permute-start = (f32[1,512]{1,0:T(1,128)S(1)}, f32[1,512]{1,0:T(1,128)S(1)}, u32[]{:S(2)}, u32[]{:S(2)}) collective-permute-start(f32[1,512]{1,0:T(1,128)S(1)} %broadcast.77), channel_id=1, source_target_pairs={{8,0},{16,8},{24,16},{9,1},{17,9},{25,17},{10,2},{18,10},{26,18},{... | collective-permute-start | bytes 6152 | tf_op jit(solution)/shard_map/ppermute | solution.py:24
  8.5 24.3 %collective-permute-start.1 = (f32[1,512]{1,0:T(1,128)S(1)}, f32[1,512]{1,0:T(1,128)S(1)}, u32[]{:S(2)}, u32[]{:S(2)}) collective-permute-start(f32[1,512]{1,0:T(1,128)S(1)} %broadcast.77), channel_id=1, source_target_pairs={{0,8},{8,16},{16,24},{1,9},{9,17},{17,25},{2,10},{10,18},{18,26},{... | collective-permute-start | bytes 6152 | tf_op jit(solution)/shard_map/ppermute | solution.py:21
  33.1 19.8 %collective-permute-start.2 = (f32[514,1]{1,0:T(8,128)S(1)}, f32[514,1]{1,0:T(8,128)S(1)}, u32[]{:S(2)}, u32[]{:S(2)}) collective-permute-start(f32[514,1]{1,0:T(8,128)S(1)} %get-tuple-element.39), channel_id=1, source_target_pairs={{1,0},{2,1},{3,2},{4,3},{5,4},{6,5},{7,6},{9,8},{10,9},{11,10},{12... | collective-permute-start | bytes 6176 | tf_op jit(solution)/shard_map/ppermute | solution.py:24
  34.4 18.5 %collective-permute-start.3 = (f32[514,1]{1,0:T(8,128)S(1)}, f32[514,1]{1,0:T(8,128)}, u32[]{:S(2)}, u32[]{:S(2)}) collective-permute-start(f32[514,1]{1,0:T(8,128)S(1)} %get-tuple-element.40), channel_id=1, source_target_pairs={{0,1},{1,2},{2,3},{3,4},{4,5},{5,6},{6,7},{8,9},{9,10},{10,11},{11... | collective-permute-start | bytes 6176 | tf_op jit(solution)/shard_map/ppermute | solution.py:21
  56.3 5.9 %collective-permute-start.4 = (f32[1,512]{1,0:T(1,128)S(1)}, f32[1,512]{1,0:T(1,128)S(1)}, u32[]{:S(2)}, u32[]{:S(2)}) collective-permute-start(f32[1,512]{1,0:T(1,128)S(1)} %get-tuple-element.48), channel_id=1, source_target_pairs={{8,0},{16,8},{24,16},{9,1},{17,9},{25,17},{10,2},{18,10},{26,18},{... | collective-permute-start | bytes 6152 | tf_op jit(solution)/shard_map/ppermute | solution.py:24
  57.6 5.8 %collective-permute-start.5 = (f32[1,512]{1,0:T(1,128)S(1)}, f32[1,512]{1,0:T(1,128)S(1)}, u32[]{:S(2)}, u32[]{:S(2)}) collective-permute-start(f32[1,512]{1,0:T(1,128)S(1)} %get-tuple-element.47), channel_id=1, source_target_pairs={{0,8},{8,16},{16,24},{1,9},{9,17},{17,25},{2,10},{10,18},{18,26},{... | collective-permute-start | bytes 6152 | tf_op jit(solution)/shard_map/ppermute | solution.py:21
  63.6 4.4 %collective-permute-start.6 = (f32[514,1]{1,0:T(8,128)S(1)}, f32[514,1]{1,0:T(8,128)S(1)}, u32[]{:S(2)}, u32[]{:S(2)}) collective-permute-start(f32[514,1]{1,0:T(8,128)S(1)} %get-tuple-element.37), channel_id=1, source_target_pairs={{1,0},{2,1},{3,2},{4,3},{5,4},{6,5},{7,6},{9,8},{10,9},{11,10},{12... | collective-permute-start | bytes 6176 | tf_op jit(solution)/shard_map/ppermute | solution.py:24
  64.9 4.2 %collective-permute-start.7 = (f32[514,1]{1,0:T(8,128)S(1)}, f32[514,1]{1,0:T(8,128)S(1)}, u32[]{:S(2)}, u32[]{:S(2)}) collective-permute-start(f32[514,1]{1,0:T(8,128)S(1)} %get-tuple-element.38), channel_id=1, source_target_pairs={{0,1},{1,2},{2,3},{3,4},{4,5},{5,6},{6,7},{8,9},{9,10},{10,11},{11... | collective-permute-start | bytes 6176 | tf_op jit(solution)/shard_map/ppermute | solution.py:21
  70.5 115.8 %copy-start.2 = (f32[512,512]{1,0:T(8,128)}, f32[512,512]{1,0:T(8,128)S(1)}, u32[]{:S(2)}) copy-start(f32[512,512]{1,0:T(8,128)S(1)} %get-tuple-element.27) | copy-start | bytes 3145732
  120.2 5.9 %collective-permute-start.8 = (f32[1,512]{1,0:T(1,128)S(1)}, f32[1,512]{1,0:T(1,128)S(1)}, u32[]{:S(2)}, u32[]{:S(2)}) collective-permute-start(f32[1,512]{1,0:T(1,128)S(1)} %get-tuple-element.46), channel_id=1, source_target_pairs={{8,0},{16,8},{24,16},{9,1},{17,9},{25,17},{10,2},{18,10},{26,18},{... | collective-permute-start | bytes 6152 | tf_op jit(solution)/shard_map/ppermute | solution.py:24
  121.5 5.8 %collective-permute-start.9 = (f32[1,512]{1,0:T(1,128)S(1)}, f32[1,512]{1,0:T(1,128)S(1)}, u32[]{:S(2)}, u32[]{:S(2)}) collective-permute-start(f32[1,512]{1,0:T(1,128)S(1)} %get-tuple-element.45), channel_id=1, source_target_pairs={{0,8},{8,16},{16,24},{1,9},{9,17},{17,25},{2,10},{10,18},{18,26},{... | collective-permute-start | bytes 6152 | tf_op jit(solution)/shard_map/ppermute | solution.py:21
  127.5 4.4 %collective-permute-start.10 = (f32[514,1]{1,0:T(8,128)S(1)}, f32[514,1]{1,0:T(8,128)S(1)}, u32[]{:S(2)}, u32[]{:S(2)}) collective-permute-start(f32[514,1]{1,0:T(8,128)S(1)} %get-tuple-element.35), channel_id=1, source_target_pairs={{1,0},{2,1},{3,2},{4,3},{5,4},{6,5},{7,6},{9,8},{10,9},{11,10},{12... | collective-permute-start | bytes 6176 | tf_op jit(solution)/shard_map/ppermute | solution.py:24
  128.8 4.2 %collective-permute-start.11 = (f32[514,1]{1,0:T(8,128)S(1)}, f32[514,1]{1,0:T(8,128)S(1)}, u32[]{:S(2)}, u32[]{:S(2)}) collective-permute-start(f32[514,1]{1,0:T(8,128)S(1)} %get-tuple-element.36), channel_id=1, source_target_pairs={{0,1},{1,2},{2,3},{3,4},{4,5},{5,6},{6,7},{8,9},{9,10},{10,11},{11... | collective-permute-start | bytes 6176 | tf_op jit(solution)/shard_map/ppermute | solution.py:21
  189.4 6.0 %collective-permute-start.12 = (f32[1,512]{1,0:T(1,128)S(1)}, f32[1,512]{1,0:T(1,128)S(1)}, u32[]{:S(2)}, u32[]{:S(2)}) collective-permute-start(f32[1,512]{1,0:T(1,128)S(1)} %get-tuple-element.44), channel_id=1, source_target_pairs={{8,0},{16,8},{24,16},{9,1},{17,9},{25,17},{10,2},{18,10},{26,18},{... | collective-permute-start | bytes 6152 | tf_op jit(solution)/shard_map/ppermute | solution.py:24
  190.7 5.8 %collective-permute-start.13 = (f32[1,512]{1,0:T(1,128)S(1)}, f32[1,512]{1,0:T(1,128)S(1)}, u32[]{:S(2)}, u32[]{:S(2)}) collective-permute-start(f32[1,512]{1,0:T(1,128)S(1)} %get-tuple-element.43), channel_id=1, source_target_pairs={{0,8},{8,16},{16,24},{1,9},{9,17},{17,25},{2,10},{10,18},{18,26},{... | collective-permute-start | bytes 6152 | tf_op jit(solution)/shard_map/ppermute | solution.py:21
  197.4 16.3 %collective-permute-start.14 = (f32[514,1]{1,0:T(8,128)}, f32[514,1]{1,0:T(8,128)S(1)}, u32[]{:S(2)}, u32[]{:S(2)}) collective-permute-start(f32[514,1]{1,0:T(8,128)} %get-tuple-element.33), channel_id=1, source_target_pairs={{1,0},{2,1},{3,2},{4,3},{5,4},{6,5},{7,6},{9,8},{10,9},{11,10},{12... | collective-permute-start | bytes 6176 | tf_op jit(solution)/shard_map/ppermute | solution.py:24
  198.7 15.0 %collective-permute-start.15 = (f32[514,1]{1,0:T(8,128)}, f32[514,1]{1,0:T(8,128)}, u32[]{:S(2)}, u32[]{:S(2)}) collective-permute-start(f32[514,1]{1,0:T(8,128)} %get-tuple-element.34), channel_id=1, source_target_pairs={{0,1},{1,2},{2,3},{3,4},{4,5},{5,6},{6,7},{8,9},{9,10},{10,11},{11... | collective-permute-start | bytes 6176 | tf_op jit(solution)/shard_map/ppermute | solution.py:21
  203.1 144.0 %collective-permute-start.23 = (f32[1,128,8]{1,2,0:T(8,128)}, f32[1,128,8]{1,2,0:T(8,128)}, u32[]{:S(2)}, u32[]{:S(2)}) collective-permute-start(f32[1,128,8]{1,2,0:T(8,128)} %bitcast.11), channel_id=1, source_target_pairs={{1,0},{2,1},{3,2},{4,3},{5,4},{6,5},{7,6},{0,7},{9,8},{10,9},{11,1... | collective-permute-start | bytes 12296 | tf_op jit(solution)/shard_map/ppermute | solution.py:24
  204.7 143.8 %collective-permute-start.22 = (f32[1,128,8]{1,2,0:T(8,128)}, f32[1,128,8]{1,2,0:T(8,128)S(1)}, u32[]{:S(2)}, u32[]{:S(2)}) collective-permute-start(f32[1,128,8]{1,2,0:T(8,128)} %bitcast.7), channel_id=1, source_target_pairs={{0,1},{1,2},{2,3},{3,4},{4,5},{5,6},{6,7},{7,0},{8,9},{9,10},{10,1... | collective-permute-start | bytes 12296 | tf_op jit(solution)/shard_map/ppermute | solution.py:21
  213.6 168.1 %reduce-scatter.3.cloned.1.call-start = ((), (), s32[]{:S(2)}) async-start(), calls=%async_computation.2 | async-start | bytes 589824 | tf_op jit(solution)/shard_map/reduce_scatter | solution.py:115
  264.6 7.7 %collective-permute-start.16 = (f32[1,512]{1,0:T(1,128)S(1)}, f32[1,512]{1,0:T(1,128)S(1)}, u32[]{:S(2)}, u32[]{:S(2)}) collective-permute-start(f32[1,512]{1,0:T(1,128)S(1)} %get-tuple-element.42), channel_id=1, source_target_pairs={{8,0},{16,8},{24,16},{9,1},{17,9},{25,17},{10,2},{18,10},{26,18},{... | collective-permute-start | bytes 6152 | tf_op jit(solution)/shard_map/ppermute | solution.py:24
  265.9 6.5 %collective-permute-start.17 = (f32[1,512]{1,0:T(1,128)S(1)}, f32[1,512]{1,0:T(1,128)S(1)}, u32[]{:S(2)}, u32[]{:S(2)}) collective-permute-start(f32[1,512]{1,0:T(1,128)S(1)} %get-tuple-element.41), channel_id=1, source_target_pairs={{0,8},{8,16},{16,24},{1,9},{9,17},{17,25},{2,10},{10,18},{18,26},{... | collective-permute-start | bytes 6152 | tf_op jit(solution)/shard_map/ppermute | solution.py:21
  271.0 77.7 %collective-permute-start.20 = (f32[1,128]{1,0:T(1,128)}, f32[1,128]{1,0:T(1,128)}, u32[]{:S(2)}, u32[]{:S(2)}) collective-permute-start(f32[1,128]{1,0:T(1,128)} %get-tuple-element.55), channel_id=1, source_target_pairs={{8,0},{16,8},{24,16},{9,1},{17,9},{25,17},{10,2},{18,10},{26,18},{... | collective-permute-start | bytes 1544 | tf_op jit(solution)/shard_map/ppermute | solution.py:24
  272.5 4.4 %collective-permute-start.18 = (f32[514,1]{1,0:T(8,128)S(1)}, f32[514,1]{1,0:T(8,128)S(1)}, u32[]{:S(2)}, u32[]{:S(2)}) collective-permute-start(f32[514,1]{1,0:T(8,128)S(1)} %get-tuple-element.31), channel_id=1, source_target_pairs={{1,0},{2,1},{3,2},{4,3},{5,4},{6,5},{7,6},{9,8},{10,9},{11,10},{12... | collective-permute-start | bytes 6176 | tf_op jit(solution)/shard_map/ppermute | solution.py:24
  273.8 8.2 %collective-permute-start.19 = (f32[514,1]{1,0:T(8,128)S(1)}, f32[514,1]{1,0:T(8,128)S(1)}, u32[]{:S(2)}, u32[]{:S(2)}) collective-permute-start(f32[514,1]{1,0:T(8,128)S(1)} %get-tuple-element.32), channel_id=1, source_target_pairs={{0,1},{1,2},{2,3},{3,4},{4,5},{5,6},{6,7},{8,9},{9,10},{10,11},{11... | collective-permute-start | bytes 6176 | tf_op jit(solution)/shard_map/ppermute | solution.py:21
  276.9 71.8 %collective-permute-start.21 = (f32[1,128]{1,0:T(1,128)}, f32[1,128]{1,0:T(1,128)}, u32[]{:S(2)}, u32[]{:S(2)}) collective-permute-start(f32[1,128]{1,0:T(1,128)} %get-tuple-element.56), channel_id=1, source_target_pairs={{0,8},{8,16},{16,24},{1,9},{9,17},{17,25},{2,10},{10,18},{18,26},{... | collective-permute-start | bytes 1544 | tf_op jit(solution)/shard_map/ppermute | solution.py:21
  348.7 44.0 %copy-start.9 = (f32[128,128]{1,0:T(8,128)S(1)}, f32[128,128]{1,0:T(8,128)}, u32[]{:S(2)}) copy-start(f32[128,128]{1,0:T(8,128)} %reduce-scatter.5.cloned.1.call-done) | copy-start | bytes 196612
  382.9 8.6 %collective-permute-start.26 = (f32[1,128,8]{1,2,0:T(8,128)S(1)}, f32[1,128,8]{1,2,0:T(8,128)S(1)}, u32[]{:S(2)}, u32[]{:S(2)}) collective-permute-start(f32[1,128,8]{1,2,0:T(8,128)S(1)} %bitcast.78), channel_id=1, source_target_pairs={{0,1},{1,2},{2,3},{3,4},{4,5},{5,6},{6,7},{7,0},{8,9},{9,10},{10,1... | collective-permute-start | bytes 12296 | tf_op jit(solution)/shard_map/ppermute | solution.py:21
  383.0 8.5 %collective-permute-start.27 = (f32[1,128,8]{1,2,0:T(8,128)S(1)}, f32[1,128,8]{1,2,0:T(8,128)S(1)}, u32[]{:S(2)}, u32[]{:S(2)}) collective-permute-start(f32[1,128,8]{1,2,0:T(8,128)S(1)} %bitcast.79), channel_id=1, source_target_pairs={{1,0},{2,1},{3,2},{4,3},{5,4},{6,5},{7,6},{0,7},{9,8},{10,9},{11,1... | collective-permute-start | bytes 12296 | tf_op jit(solution)/shard_map/ppermute | solution.py:24
  385.6 6.1 %collective-permute-start.24 = (f32[1,128]{1,0:T(1,128)S(1)}, f32[1,128]{1,0:T(1,128)S(1)}, u32[]{:S(2)}, u32[]{:S(2)}) collective-permute-start(f32[1,128]{1,0:T(1,128)S(1)} %get-tuple-element.49), channel_id=1, source_target_pairs={{8,0},{16,8},{24,16},{9,1},{17,9},{25,17},{10,2},{18,10},{26,18},{... | collective-permute-start | bytes 1544 | tf_op jit(solution)/shard_map/ppermute | solution.py:24
  386.9 5.8 %collective-permute-start.25 = (f32[1,128]{1,0:T(1,128)S(1)}, f32[1,128]{1,0:T(1,128)S(1)}, u32[]{:S(2)}, u32[]{:S(2)}) collective-permute-start(f32[1,128]{1,0:T(1,128)S(1)} %get-tuple-element.50), channel_id=1, source_target_pairs={{0,8},{8,16},{16,24},{1,9},{9,17},{17,25},{2,10},{10,18},{18,26},{... | collective-permute-start | bytes 1544 | tf_op jit(solution)/shard_map/ppermute | solution.py:21
  (16 other events, 178.6 us)
Sparse Core Ops, SparseCore 0:
  213.8 36.5 reduce-scatter.4
  347.2 34.5 reduce-scatter.2
where the time goes:
time: 402 us; the launch traced here: 400 us
  blocking collectives  190 us (47%)
  starting transfers between devices  69.9 us (17%)
  other arithmetic  50.6 us (13%)
  waiting for transfers between devices  40.1 us (10%)
  between operations  28.2 us (7%)
  local copies, waits for them, and re-layouts  21.2 us (5%)
    psum x4, blocking collectives, paired_sum(): return lax.psum((jnp.sum(first), jnp.sum(second)), ('row', 'col'))  179 us
    ppermute x14, starting transfers between devices, extended(): lax.ppermute(lax.slice_in_dim(block, block.shape[dim] - width, None, axis...  50.1 us
    reduce_scatter x1, waiting for transfers between devices, per_device(): lax.psum_scatter(partial_block.reshape(block_rows, row_width), 'col', sca...  33 us
    ppermute x14, starting transfers between devices, extended(): lax.ppermute(lax.slice_in_dim(block, 0, width, axis=dim), axis, backward)  19.7 us
    all_gather x1, blocking collectives, per_device(): gathered = lax.all_gather(volt, 'col', axis=1, tiled=True)  11.7 us
    div x4, other arithmetic, per_device(): precond = residual / fine_diag  10.8 us
  transfers between devices with their start and end apart: 30, of which 7 were waited for; matrix products, arithmetic and copies ran while one was open for 14% of the time, Pallas kernels for 0%

commit v1 on v0

--- a/solution.py
+++ b/solution.py
@@ -59,7 +59,7 @@
 
 
 def paired_sum(first, second):
-    return lax.psum((jnp.sum(first), jnp.sum(second)), ("row", "col"))
+    return lax.psum(lax.psum((jnp.sum(first), jnp.sum(second)), "row"), "col")
 
 
 def per_device(

time: 402 us -> 331 us (0.82)
  blocking collectives: 190 us -> 122 us
    psum x4 -> x8, blocking collectives: 179 us -> 110 us  [paired_sum(): return lax.psum(lax.psum((jnp.sum(first), jnp.sum(second)), 'row'), 'col')]
  transfers between devices with their start and end apart: 30 -> 30, of which waited for: 7 -> 7; matrix products, arithmetic and copies ran while one was open for 14% -> 17% of each run, Pallas kernels for 0% -> 0%
where the time goes in v1:
time: 331 us; the launch traced here: 330 us
  blocking collectives  122 us (37%)
  starting transfers between devices  69 us (21%)
  other arithmetic  50.6 us (15%)
  waiting for transfers between devices  39.2 us (12%)
  between operations  28.2 us (9%)
  local copies, waits for them, and re-layouts  21.1 us (6%)
    psum x8, blocking collectives, paired_sum(): return lax.psum(lax.psum((jnp.sum(first), jnp.sum(second)), 'row'), 'col')  110 us
    ppermute x14, starting transfers between devices, extended(): lax.ppermute(lax.slice_in_dim(block, block.shape[dim] - width, None, axis...  50.7 us
    reduce_scatter x1, waiting for transfers between devices, per_device(): lax.psum_scatter(partial_block.reshape(block_rows, row_width), 'col', sca...  32.1 us
    ppermute x14, starting transfers between devices, extended(): lax.ppermute(lax.slice_in_dim(block, 0, width, axis=dim), axis, backward)  18.1 us
    all_gather x1, blocking collectives, per_device(): gathered = lax.all_gather(volt, 'col', axis=1, tiled=True)  11.7 us
    div x4, other arithmetic, per_device(): precond = residual / fine_diag  10.8 us
    reduce_sum x4, other arithmetic, paired_sum(): return lax.psum(lax.psum((jnp.sum(first), jnp.sum(second)), 'row'), 'col')  7.65 us
    ppermute x14, waiting for transfers between devices, extended(): lax.ppermute(lax.slice_in_dim(block, block.shape[dim] - width, None, axis...  6.97 us
  transfers between devices with their start and end apart: 30, of which 7 were waited for; matrix products, arithmetic and copies ran while one was open for 17% of the time, Pallas kernels for 0%

profile of v1, /device:TPU:0, one launch (start us, length us, event | category | flops | bytes accessed | tf_op | source)
XLA Modules:
  0.0 329.7 jit_solution(10402858804544568571)
XLA Ops:
  8.5 5.6 %collective-permute-start.1 = (f32[1,512]{1,0:T(1,128)S(1)}, f32[1,512]{1,0:T(1,128)S(1)}, u32[]{:S(2)}, u32[]{:S(2)}) collective-permute-start(f32[1,512]{1,0:T(1,128)S(1)} %broadcast.77), channel_id=1, source_target_pairs={{0,8},{8,16},{16,24},{1,9},{9,17},{17,25},{2,10},{10,18},{18,26},{... | collective-permute-start | bytes 6152 | tf_op jit(solution)/shard_map/ppermute | solution.py:21
  14.8 11.7 %all_gather.3 = f32[128,1024]{1,0:T(8,128)S(1)} all-gather(f32[128,128]{1,0:T(8,128)} %param.12), channel_id=1, replica_groups=mesh['row'=4,'col'=8] {'col'}, dimensions={1}, use_global_device_ids=true | all-gather | bytes 589824 | tf_op jit(solution)/shard_map/all_gather | solution.py:90
  26.6 6.2 %gather_fusion = f32[1024]{0:T(1024)S(1)} fusion(f32[131072]{0:T(1024)S(1)} %bitcast.53, s32[1024]{0:T(1024)S(1)} %broadcast_clamp_fusion.1), kind=kCustom, calls=%fused_computation | custom fusion | bytes 12288 | tf_op jit(solution)/shard_map/gather | solution.py:91
  34.4 3.8 %collective-permute-start.3 = (f32[514,1]{1,0:T(8,128)S(1)}, f32[514,1]{1,0:T(8,128)}, u32[]{:S(2)}, u32[]{:S(2)}) collective-permute-start(f32[514,1]{1,0:T(8,128)S(1)} %get-tuple-element.48), channel_id=1, source_target_pairs={{0,1},{1,2},{2,3},{3,4},{4,5},{5,6},{6,7},{8,9},{9,10},{10,11},{11... | collective-permute-start | bytes 6176 | tf_op jit(solution)/shard_map/ppermute | solution.py:21
  38.2 6.2 %scatter_custom_fusion.1 = f32[262144]{0:T(1024)S(1)} fusion(s32[1024]{0:T(1024)S(1)} %bitcast.75, f32[1024]{0:T(1024)S(1)} %get-tuple-element.69, f32[]{:T(128)} %constant.12.clone.1), kind=kCustom, calls=%fused_computation.82 | custom fusion | flops 1024 | bytes 1048580 | tf_op jit(solution)/shard_map/scatter-add | solution.py:80
  45.6 6.2 %scatter_custom_fusion = f32[262144]{0:T(1024)S(1)} fusion(s32[1024]{0:T(1024)S(1)} %bitcast.76, f32[1024]{0:T(1024)S(1)} %get-tuple-element.70, f32[]{:T(128)} %constant.12.clone.1), kind=kCustom, calls=%fused_computation.84 | custom fusion | flops 1024 | bytes 1048580 | tf_op jit(solution)/shard_map/scatter-add | solution.py:92
  52.9 3.4 %fusion.61 = (f32[512,512]{1,0:T(8,128)S(1)}, f32[512,512]{1,0:T(8,128)S(1)}, f32[512,512]{1,0:T(8,128)S(1)}) fusion(f32[1,512]{1,0:T(1,128)S(1)} %collective-permute-done, f32[512,512]{1,0:T(8,128)S(1)} %broadcast_in_dim.35, f32[1,512]{1,0:T(1,128)S(1)} %collective-permute-done.1, f32[514,1]{1,0:T(8,128)} %collective-permute-done.3, ...), kind=kLoop, calls=%fused_computation.152 | loop fusion | flops 4718592 | bytes 9445392 | tf_op jit(solution)/shard_map/div | solution.py:95
  57.6 4.5 %collective-permute-start.5 = (f32[1,512]{1,0:T(1,128)S(1)}, f32[1,512]{1,0:T(1,128)S(1)}, u32[]{:S(2)}, u32[]{:S(2)}) collective-permute-start(f32[1,512]{1,0:T(1,128)S(1)} %get-tuple-element.55), channel_id=1, source_target_pairs={{0,8},{8,16},{16,24},{1,9},{9,17},{17,25},{2,10},{10,18},{18,26},{... | collective-permute-start | bytes 6152 | tf_op jit(solution)/shard_map/ppermute | solution.py:21
  64.9 3.0 collective-permute-start.7
  70.5 13.4 %all-reduce.13 = (f32[]{:T(128)}, f32[]{:T(128)}) all-reduce(f32[]{:T(128)} %get-tuple-element.11, f32[]{:T(128)} %get-tuple-element.10), channel_id=1, replica_groups=mesh['row'=4,'col'=8] {'row'}, use_global_device_ids=true, to_apply=%region_3.4 | all-reduce | flops 2 | bytes 16 | tf_op jit(solution)/shard_map/psum | solution.py:62
  83.9 17.1 %all-reduce.9 = (f32[]{:T(128)}, f32[]{:T(128)}) all-reduce(f32[]{:T(128)} %get-tuple-element.26, f32[]{:T(128)} %get-tuple-element.27), channel_id=1, replica_groups=mesh['row'=4,'col'=8] {'col'}, use_global_device_ids=true, to_apply=%region_4.5 | all-reduce | flops 2 | bytes 16 | tf_op jit(solution)/shard_map/psum | solution.py:62
  105.2 4.5 %collective-permute-start.9 = (f32[1,512]{1,0:T(1,128)S(1)}, f32[1,512]{1,0:T(1,128)S(1)}, u32[]{:S(2)}, u32[]{:S(2)}) collective-permute-start(f32[1,512]{1,0:T(1,128)S(1)} %get-tuple-element.53), channel_id=1, source_target_pairs={{0,8},{8,16},{16,24},{1,9},{9,17},{17,25},{2,10},{10,18},{18,26},{... | collective-permute-start | bytes 6152 | tf_op jit(solution)/shard_map/ppermute | solution.py:21
  112.5 3.0 collective-permute-start.11
  119.1 11.2 %all-reduce.12 = (f32[]{:T(128)}, f32[]{:T(128)}) all-reduce(f32[]{:T(128)} %get-tuple-element.9, f32[]{:T(128)} %get-tuple-element.8), channel_id=1, replica_groups=mesh['row'=4,'col'=8] {'row'}, use_global_device_ids=true, to_apply=%region_9.10 | all-reduce | flops 2 | bytes 16 | tf_op jit(solution)/shard_map/psum | solution.py:62
  130.3 17.6 %all-reduce.8 = (f32[]{:T(128)}, f32[]{:T(128)}) all-reduce(f32[]{:T(128)} %get-tuple-element.24, f32[]{:T(128)} %get-tuple-element.25), channel_id=1, replica_groups=mesh['row'=4,'col'=8] {'col'}, use_global_device_ids=true, to_apply=%region_10.11 | all-reduce | flops 2 | bytes 16 | tf_op jit(solution)/shard_map/psum | solution.py:62
  152.3 3.0 fusion.57
  156.6 4.5 %collective-permute-start.13 = (f32[1,512]{1,0:T(1,128)S(1)}, f32[1,512]{1,0:T(1,128)S(1)}, u32[]{:S(2)}, u32[]{:S(2)}) collective-permute-start(f32[1,512]{1,0:T(1,128)S(1)} %get-tuple-element.51), channel_id=1, source_target_pairs={{0,8},{8,16},{16,24},{1,9},{9,17},{17,25},{2,10},{10,18},{18,26},{... | collective-permute-start | bytes 6152 | tf_op jit(solution)/shard_map/ppermute | solution.py:21
  164.6 3.8 %collective-permute-start.15 = (f32[514,1]{1,0:T(8,128)}, f32[514,1]{1,0:T(8,128)}, u32[]{:S(2)}, u32[]{:S(2)}) collective-permute-start(f32[514,1]{1,0:T(8,128)} %get-tuple-element.42), channel_id=1, source_target_pairs={{0,1},{1,2},{2,3},{3,4},{4,5},{5,6},{6,7},{8,9},{9,10},{10,11},{11... | collective-permute-start | bytes 6176 | tf_op jit(solution)/shard_map/ppermute | solution.py:21
  169.5 6.9 %scatter_custom_fusion.3 = f32[131072]{0:T(1024)} fusion(s32[1024]{0:T(1024)} %bitcast.73, f32[1024]{0:T(1024)} %copy-done.14, f32[]{:T(128)} %constant.12.clone.1), kind=kCustom, calls=%fused_computation.101 | custom fusion | flops 1024 | bytes 524800 | tf_op jit(solution)/shard_map/scatter-add | solution.py:82
  180.9 11.4 %all-reduce.11 = (f32[]{:T(128)}, f32[]{:T(128)}) all-reduce(f32[]{:T(128)} %get-tuple-element.7, f32[]{:T(128)} %get-tuple-element.6), channel_id=1, replica_groups=mesh['row'=4,'col'=8] {'row'}, use_global_device_ids=true, to_apply=%region_15.16 | all-reduce | flops 2 | bytes 16 | tf_op jit(solution)/shard_map/psum | solution.py:62
  192.3 13.0 %all-reduce.7 = (f32[]{:T(128)}, f32[]{:T(128)}) all-reduce(f32[]{:T(128)} %get-tuple-element.22, f32[]{:T(128)} %get-tuple-element.23), channel_id=1, replica_groups=mesh['row'=4,'col'=8] {'col'}, use_global_device_ids=true, to_apply=%region_16.17 | all-reduce | flops 2 | bytes 16 | tf_op jit(solution)/shard_map/psum | solution.py:62
  209.3 2.8 fusion.56
  213.4 4.5 %collective-permute-start.17 = (f32[1,512]{1,0:T(1,128)S(1)}, f32[1,512]{1,0:T(1,128)S(1)}, u32[]{:S(2)}, u32[]{:S(2)}) collective-permute-start(f32[1,512]{1,0:T(1,128)S(1)} %get-tuple-element.49), channel_id=1, source_target_pairs={{0,8},{8,16},{16,24},{1,9},{9,17},{17,25},{2,10},{10,18},{18,26},{... | collective-permute-start | bytes 6152 | tf_op jit(solution)/shard_map/ppermute | solution.py:21
  221.2 3.0 collective-permute-start.19
  224.3 5.1 %collective-permute-start.21 = (f32[1,128]{1,0:T(1,128)}, f32[1,128]{1,0:T(1,128)}, u32[]{:S(2)}, u32[]{:S(2)}) collective-permute-start(f32[1,128]{1,0:T(1,128)} %get-tuple-element.64), channel_id=1, source_target_pairs={{0,8},{8,16},{16,24},{1,9},{9,17},{17,25},{2,10},{10,18},{18,26},{... | collective-permute-start | bytes 1544 | tf_op jit(solution)/shard_map/ppermute | solution.py:21
  230.9 9.0 %all-reduce.10 = (f32[]{:T(128)}, f32[]{:T(128)}) all-reduce(f32[]{:T(128)} %get-tuple-element.5, f32[]{:T(128)} %get-tuple-element.4), channel_id=1, replica_groups=mesh['row'=4,'col'=8] {'row'}, use_global_device_ids=true, to_apply=%region_21.22 | all-reduce | flops 2 | bytes 16 | tf_op jit(solution)/shard_map/psum | solution.py:62
  239.9 17.2 %all-reduce.6 = (f32[]{:T(128)}, f32[]{:T(128)}) all-reduce(f32[]{:T(128)} %get-tuple-element.20, f32[]{:T(128)} %get-tuple-element.21), channel_id=1, replica_groups=mesh['row'=4,'col'=8] {'col'}, use_global_device_ids=true, to_apply=%region_22.23 | all-reduce | flops 2 | bytes 16 | tf_op jit(solution)/shard_map/psum | solution.py:62
  264.0 6.1 %gather_fusion.1 = f32[1024]{0:T(1024)S(1)} fusion(f32[262144]{0:T(1024)S(1)} %bitcast.54, s32[1024]{0:T(1024)S(1)} %broadcast_clamp_fusion), kind=kCustom, calls=%fused_computation.1 | custom fusion | bytes 12288 | tf_op jit(solution)/shard_map/gather | solution.py:113
  270.3 6.2 %scatter_custom_fusion.2 = f32[131072]{0:T(1024)S(1)} fusion(s32[1024]{0:T(1024)} %bitcast.74, f32[1024]{0:T(1024)S(1)} %fusion.54, f32[]{:T(128)} %constant.12.clone.1), kind=kCustom, calls=%fused_computation.103 | custom fusion | flops 1024 | bytes 524800 | tf_op jit(solution)/shard_map/scatter-add | solution.py:114
  279.1 32.1 %reduce-scatter.3.cloned.1.call-done = f32[128,128]{1,0:T(8,128)} async-done(((f32[128,1024]{1,0:T(8,128)}), f32[128,128]{1,0:T(8,128)}) %reduce-scatter.3.cloned.1.call-update) | async-done | bytes 65552 | tf_op jit(solution)/shard_map/reduce_scatter | solution.py:115
  312.4 2.6 collective-permute-start.27
  316.3 4.5 %collective-permute-start.25 = (f32[1,128]{1,0:T(1,128)S(1)}, f32[1,128]{1,0:T(1,128)S(1)}, u32[]{:S(2)}, u32[]{:S(2)}) collective-permute-start(f32[1,128]{1,0:T(1,128)S(1)} %get-tuple-element.58), channel_id=1, source_target_pairs={{0,8},{8,16},{16,24},{1,9},{9,17},{17,25},{2,10},{10,18},{18,26},{... | collective-permute-start | bytes 1544 | tf_op jit(solution)/shard_map/ppermute | solution.py:21
  (136 shorter events, 48.1 us)
Async XLA Ops:
  7.2 271.9 %reduce-scatter.5.cloned.1.call-start = ((), (), s32[]{:S(2)}) async-start(), calls=%async_computation.3 | async-start | bytes 589824 | tf_op jit(solution)/shard_map/reduce_scatter | solution.py:83
  7.2 25.6 %collective-permute-start = (f32[1,512]{1,0:T(1,128)S(1)}, f32[1,512]{1,0:T(1,128)S(1)}, u32[]{:S(2)}, u32[]{:S(2)}) collective-permute-start(f32[1,512]{1,0:T(1,128)S(1)} %broadcast.77), channel_id=1, source_target_pairs={{8,0},{16,8},{24,16},{9,1},{17,9},{25,17},{10,2},{18,10},{26,18},{... | collective-permute-start | bytes 6152 | tf_op jit(solution)/shard_map/ppermute | solution.py:24
  8.5 24.3 %collective-permute-start.1 = (f32[1,512]{1,0:T(1,128)S(1)}, f32[1,512]{1,0:T(1,128)S(1)}, u32[]{:S(2)}, u32[]{:S(2)}) collective-permute-start(f32[1,512]{1,0:T(1,128)S(1)} %broadcast.77), channel_id=1, source_target_pairs={{0,8},{8,16},{16,24},{1,9},{9,17},{17,25},{2,10},{10,18},{18,26},{... | collective-permute-start | bytes 6152 | tf_op jit(solution)/shard_map/ppermute | solution.py:21
  33.1 19.7 %collective-permute-start.2 = (f32[514,1]{1,0:T(8,128)S(1)}, f32[514,1]{1,0:T(8,128)S(1)}, u32[]{:S(2)}, u32[]{:S(2)}) collective-permute-start(f32[514,1]{1,0:T(8,128)S(1)} %get-tuple-element.47), channel_id=1, source_target_pairs={{1,0},{2,1},{3,2},{4,3},{5,4},{6,5},{7,6},{9,8},{10,9},{11,10},{12... | collective-permute-start | bytes 6176 | tf_op jit(solution)/shard_map/ppermute | solution.py:24
  34.4 18.4 %collective-permute-start.3 = (f32[514,1]{1,0:T(8,128)S(1)}, f32[514,1]{1,0:T(8,128)}, u32[]{:S(2)}, u32[]{:S(2)}) collective-permute-start(f32[514,1]{1,0:T(8,128)S(1)} %get-tuple-element.48), channel_id=1, source_target_pairs={{0,1},{1,2},{2,3},{3,4},{4,5},{5,6},{6,7},{8,9},{9,10},{10,11},{11... | collective-permute-start | bytes 6176 | tf_op jit(solution)/shard_map/ppermute | solution.py:21
  56.3 5.9 %collective-permute-start.4 = (f32[1,512]{1,0:T(1,128)S(1)}, f32[1,512]{1,0:T(1,128)S(1)}, u32[]{:S(2)}, u32[]{:S(2)}) collective-permute-start(f32[1,512]{1,0:T(1,128)S(1)} %get-tuple-element.56), channel_id=1, source_target_pairs={{8,0},{16,8},{24,16},{9,1},{17,9},{25,17},{10,2},{18,10},{26,18},{... | collective-permute-start | bytes 6152 | tf_op jit(solution)/shard_map/ppermute | solution.py:24
  57.6 5.8 %collective-permute-start.5 = (f32[1,512]{1,0:T(1,128)S(1)}, f32[1,512]{1,0:T(1,128)S(1)}, u32[]{:S(2)}, u32[]{:S(2)}) collective-permute-start(f32[1,512]{1,0:T(1,128)S(1)} %get-tuple-element.55), channel_id=1, source_target_pairs={{0,8},{8,16},{16,24},{1,9},{9,17},{17,25},{2,10},{10,18},{18,26},{... | collective-permute-start | bytes 6152 | tf_op jit(solution)/shard_map/ppermute | solution.py:21
  63.6 4.4 %collective-permute-start.6 = (f32[514,1]{1,0:T(8,128)S(1)}, f32[514,1]{1,0:T(8,128)S(1)}, u32[]{:S(2)}, u32[]{:S(2)}) collective-permute-start(f32[514,1]{1,0:T(8,128)S(1)} %get-tuple-element.45), channel_id=1, source_target_pairs={{1,0},{2,1},{3,2},{4,3},{5,4},{6,5},{7,6},{9,8},{10,9},{11,10},{12... | collective-permute-start | bytes 6176 | tf_op jit(solution)/shard_map/ppermute | solution.py:24
  64.9 4.2 %collective-permute-start.7 = (f32[514,1]{1,0:T(8,128)S(1)}, f32[514,1]{1,0:T(8,128)S(1)}, u32[]{:S(2)}, u32[]{:S(2)}) collective-permute-start(f32[514,1]{1,0:T(8,128)S(1)} %get-tuple-element.46), channel_id=1, source_target_pairs={{0,1},{1,2},{2,3},{3,4},{4,5},{5,6},{6,7},{8,9},{9,10},{10,11},{11... | collective-permute-start | bytes 6176 | tf_op jit(solution)/shard_map/ppermute | solution.py:21
  70.5 81.7 %copy-start.2 = (f32[512,512]{1,0:T(8,128)}, f32[512,512]{1,0:T(8,128)S(1)}, u32[]{:S(2)}) copy-start(f32[512,512]{1,0:T(8,128)S(1)} %get-tuple-element.35) | copy-start | bytes 3145732
  103.9 5.9 %collective-permute-start.8 = (f32[1,512]{1,0:T(1,128)S(1)}, f32[1,512]{1,0:T(1,128)S(1)}, u32[]{:S(2)}, u32[]{:S(2)}) collective-permute-start(f32[1,512]{1,0:T(1,128)S(1)} %get-tuple-element.54), channel_id=1, source_target_pairs={{8,0},{16,8},{24,16},{9,1},{17,9},{25,17},{10,2},{18,10},{26,18},{... | collective-permute-start | bytes 6152 | tf_op jit(solution)/shard_map/ppermute | solution.py:24
  105.2 5.8 %collective-permute-start.9 = (f32[1,512]{1,0:T(1,128)S(1)}, f32[1,512]{1,0:T(1,128)S(1)}, u32[]{:S(2)}, u32[]{:S(2)}) collective-permute-start(f32[1,512]{1,0:T(1,128)S(1)} %get-tuple-element.53), channel_id=1, source_target_pairs={{0,8},{8,16},{16,24},{1,9},{9,17},{17,25},{2,10},{10,18},{18,26},{... | collective-permute-start | bytes 6152 | tf_op jit(solution)/shard_map/ppermute | solution.py:21
  111.2 4.4 %collective-permute-start.10 = (f32[514,1]{1,0:T(8,128)S(1)}, f32[514,1]{1,0:T(8,128)S(1)}, u32[]{:S(2)}, u32[]{:S(2)}) collective-permute-start(f32[514,1]{1,0:T(8,128)S(1)} %get-tuple-element.43), channel_id=1, source_target_pairs={{1,0},{2,1},{3,2},{4,3},{5,4},{6,5},{7,6},{9,8},{10,9},{11,10},{12... | collective-permute-start | bytes 6176 | tf_op jit(solution)/shard_map/ppermute | solution.py:24
  112.5 4.2 %collective-permute-start.11 = (f32[514,1]{1,0:T(8,128)S(1)}, f32[514,1]{1,0:T(8,128)S(1)}, u32[]{:S(2)}, u32[]{:S(2)}) collective-permute-start(f32[514,1]{1,0:T(8,128)S(1)} %get-tuple-element.44), channel_id=1, source_target_pairs={{0,1},{1,2},{2,3},{3,4},{4,5},{5,6},{6,7},{8,9},{9,10},{10,11},{11... | collective-permute-start | bytes 6176 | tf_op jit(solution)/shard_map/ppermute | solution.py:21
  155.3 6.0 %collective-permute-start.12 = (f32[1,512]{1,0:T(1,128)S(1)}, f32[1,512]{1,0:T(1,128)S(1)}, u32[]{:S(2)}, u32[]{:S(2)}) collective-permute-start(f32[1,512]{1,0:T(1,128)S(1)} %get-tuple-element.52), channel_id=1, source_target_pairs={{8,0},{16,8},{24,16},{9,1},{17,9},{25,17},{10,2},{18,10},{26,18},{... | collective-permute-start | bytes 6152 | tf_op jit(solution)/shard_map/ppermute | solution.py:24
  156.6 5.8 %collective-permute-start.13 = (f32[1,512]{1,0:T(1,128)S(1)}, f32[1,512]{1,0:T(1,128)S(1)}, u32[]{:S(2)}, u32[]{:S(2)}) collective-permute-start(f32[1,512]{1,0:T(1,128)S(1)} %get-tuple-element.51), channel_id=1, source_target_pairs={{0,8},{8,16},{16,24},{1,9},{9,17},{17,25},{2,10},{10,18},{18,26},{... | collective-permute-start | bytes 6152 | tf_op jit(solution)/shard_map/ppermute | solution.py:21
  163.3 15.2 %collective-permute-start.14 = (f32[514,1]{1,0:T(8,128)}, f32[514,1]{1,0:T(8,128)S(1)}, u32[]{:S(2)}, u32[]{:S(2)}) collective-permute-start(f32[514,1]{1,0:T(8,128)} %get-tuple-element.41), channel_id=1, source_target_pairs={{1,0},{2,1},{3,2},{4,3},{5,4},{6,5},{7,6},{9,8},{10,9},{11,10},{12... | collective-permute-start | bytes 6176 | tf_op jit(solution)/shard_map/ppermute | solution.py:24
  164.6 13.9 %collective-permute-start.15 = (f32[514,1]{1,0:T(8,128)}, f32[514,1]{1,0:T(8,128)}, u32[]{:S(2)}, u32[]{:S(2)}) collective-permute-start(f32[514,1]{1,0:T(8,128)} %get-tuple-element.42), channel_id=1, source_target_pairs={{0,1},{1,2},{2,3},{3,4},{4,5},{5,6},{6,7},{8,9},{9,10},{10,11},{11... | collective-permute-start | bytes 6176 | tf_op jit(solution)/shard_map/ppermute | solution.py:21
  169.0 108.4 %collective-permute-start.23 = (f32[1,128,8]{1,2,0:T(8,128)}, f32[1,128,8]{1,2,0:T(8,128)}, u32[]{:S(2)}, u32[]{:S(2)}) collective-permute-start(f32[1,128,8]{1,2,0:T(8,128)} %bitcast.11), channel_id=1, source_target_pairs={{1,0},{2,1},{3,2},{4,3},{5,4},{6,5},{7,6},{0,7},{9,8},{10,9},{11,1... | collective-permute-start | bytes 12296 | tf_op jit(solution)/shard_map/ppermute | solution.py:24
  169.0 109.8 %collective-permute-start.22 = (f32[1,128,8]{1,2,0:T(8,128)}, f32[1,128,8]{1,2,0:T(8,128)S(1)}, u32[]{:S(2)}, u32[]{:S(2)}) collective-permute-start(f32[1,128,8]{1,2,0:T(8,128)} %bitcast.7), channel_id=1, source_target_pairs={{0,1},{1,2},{2,3},{3,4},{4,5},{5,6},{6,7},{7,0},{8,9},{9,10},{10,1... | collective-permute-start | bytes 12296 | tf_op jit(solution)/shard_map/ppermute | solution.py:21
  178.3 132.9 %reduce-scatter.3.cloned.1.call-start = ((), (), s32[]{:S(2)}) async-start(), calls=%async_computation.2 | async-start | bytes 589824 | tf_op jit(solution)/shard_map/reduce_scatter | solution.py:115
  212.1 7.7 %collective-permute-start.16 = (f32[1,512]{1,0:T(1,128)S(1)}, f32[1,512]{1,0:T(1,128)S(1)}, u32[]{:S(2)}, u32[]{:S(2)}) collective-permute-start(f32[1,512]{1,0:T(1,128)S(1)} %get-tuple-element.50), channel_id=1, source_target_pairs={{8,0},{16,8},{24,16},{9,1},{17,9},{25,17},{10,2},{18,10},{26,18},{... | collective-permute-start | bytes 6152 | tf_op jit(solution)/shard_map/ppermute | solution.py:24
  213.4 6.4 %collective-permute-start.17 = (f32[1,512]{1,0:T(1,128)S(1)}, f32[1,512]{1,0:T(1,128)S(1)}, u32[]{:S(2)}, u32[]{:S(2)}) collective-permute-start(f32[1,512]{1,0:T(1,128)S(1)} %get-tuple-element.49), channel_id=1, source_target_pairs={{0,8},{8,16},{16,24},{1,9},{9,17},{17,25},{2,10},{10,18},{18,26},{... | collective-permute-start | bytes 6152 | tf_op jit(solution)/shard_map/ppermute | solution.py:21
  218.5 60.5 %collective-permute-start.20 = (f32[1,128]{1,0:T(1,128)}, f32[1,128]{1,0:T(1,128)}, u32[]{:S(2)}, u32[]{:S(2)}) collective-permute-start(f32[1,128]{1,0:T(1,128)} %get-tuple-element.63), channel_id=1, source_target_pairs={{8,0},{16,8},{24,16},{9,1},{17,9},{25,17},{10,2},{18,10},{26,18},{... | collective-permute-start | bytes 1544 | tf_op jit(solution)/shard_map/ppermute | solution.py:24
  219.9 4.4 %collective-permute-start.18 = (f32[514,1]{1,0:T(8,128)S(1)}, f32[514,1]{1,0:T(8,128)S(1)}, u32[]{:S(2)}, u32[]{:S(2)}) collective-permute-start(f32[514,1]{1,0:T(8,128)S(1)} %get-tuple-element.39), channel_id=1, source_target_pairs={{1,0},{2,1},{3,2},{4,3},{5,4},{6,5},{7,6},{9,8},{10,9},{11,10},{12... | collective-permute-start | bytes 6176 | tf_op jit(solution)/shard_map/ppermute | solution.py:24
  221.2 8.2 %collective-permute-start.19 = (f32[514,1]{1,0:T(8,128)S(1)}, f32[514,1]{1,0:T(8,128)S(1)}, u32[]{:S(2)}, u32[]{:S(2)}) collective-permute-start(f32[514,1]{1,0:T(8,128)S(1)} %get-tuple-element.40), channel_id=1, source_target_pairs={{0,1},{1,2},{2,3},{3,4},{4,5},{5,6},{6,7},{8,9},{9,10},{10,11},{11... | collective-permute-start | bytes 6176 | tf_op jit(solution)/shard_map/ppermute | solution.py:21
  224.3 54.7 %collective-permute-start.21 = (f32[1,128]{1,0:T(1,128)}, f32[1,128]{1,0:T(1,128)}, u32[]{:S(2)}, u32[]{:S(2)}) collective-permute-start(f32[1,128]{1,0:T(1,128)} %get-tuple-element.64), channel_id=1, source_target_pairs={{0,8},{8,16},{16,24},{1,9},{9,17},{17,25},{2,10},{10,18},{18,26},{... | collective-permute-start | bytes 1544 | tf_op jit(solution)/shard_map/ppermute | solution.py:21
  279.1 43.1 %copy-start.9 = (f32[128,128]{1,0:T(8,128)S(1)}, f32[128,128]{1,0:T(8,128)}, u32[]{:S(2)}) copy-start(f32[128,128]{1,0:T(8,128)} %reduce-scatter.5.cloned.1.call-done) | copy-start | bytes 196612
  312.3 8.6 %collective-permute-start.26 = (f32[1,128,8]{1,2,0:T(8,128)S(1)}, f32[1,128,8]{1,2,0:T(8,128)S(1)}, u32[]{:S(2)}, u32[]{:S(2)}) collective-permute-start(f32[1,128,8]{1,2,0:T(8,128)S(1)} %bitcast.78), channel_id=1, source_target_pairs={{0,1},{1,2},{2,3},{3,4},{4,5},{5,6},{6,7},{7,0},{8,9},{9,10},{10,1... | collective-permute-start | bytes 12296 | tf_op jit(solution)/shard_map/ppermute | solution.py:21
  312.4 8.5 %collective-permute-start.27 = (f32[1,128,8]{1,2,0:T(8,128)S(1)}, f32[1,128,8]{1,2,0:T(8,128)S(1)}, u32[]{:S(2)}, u32[]{:S(2)}) collective-permute-start(f32[1,128,8]{1,2,0:T(8,128)S(1)} %bitcast.79), channel_id=1, source_target_pairs={{1,0},{2,1},{3,2},{4,3},{5,4},{6,5},{7,6},{0,7},{9,8},{10,9},{11,1... | collective-permute-start | bytes 12296 | tf_op jit(solution)/shard_map/ppermute | solution.py:24
  315.0 6.1 %collective-permute-start.24 = (f32[1,128]{1,0:T(1,128)S(1)}, f32[1,128]{1,0:T(1,128)S(1)}, u32[]{:S(2)}, u32[]{:S(2)}) collective-permute-start(f32[1,128]{1,0:T(1,128)S(1)} %get-tuple-element.57), channel_id=1, source_target_pairs={{8,0},{16,8},{24,16},{9,1},{17,9},{25,17},{10,2},{18,10},{26,18},{... | collective-permute-start | bytes 1544 | tf_op jit(solution)/shard_map/ppermute | solution.py:24
  316.3 5.8 %collective-permute-start.25 = (f32[1,128]{1,0:T(1,128)S(1)}, f32[1,128]{1,0:T(1,128)S(1)}, u32[]{:S(2)}, u32[]{:S(2)}) collective-permute-start(f32[1,128]{1,0:T(1,128)S(1)} %get-tuple-element.58), channel_id=1, source_target_pairs={{0,8},{8,16},{16,24},{1,9},{9,17},{17,25},{2,10},{10,18},{18,26},{... | collective-permute-start | bytes 1544 | tf_op jit(solution)/shard_map/ppermute | solution.py:21
  (16 other events, 178.3 us)
Sparse Core Ops, SparseCore 0:
  178.4 36.7 reduce-scatter.4
  277.5 33.6 reduce-scatter.2
